TPU v7x, 32 devices: a whole 2x2x4 slice. The times are simulated.
32 devices in a mesh: cfg: 2 (over y), space: 8 (over z, x), tm: 2 (over core).
Axes of the slice: x: 2, y: 2, z: 4, core: 2. Of those that a mesh axis runs over, the one named last changes fastest.
Arguments:
- eigvecs: bfloat16 [4, 2, 3, 1536, 256], P(('cfg', 'tm'), None, None, 'space'), parts along dimension 0, may hold values from -6 to 6
- momenta: int32 [3, 3], replicated, may hold values from -2 to 2, as said below
- pair_list: int32 [8, 2], P('tm'), may hold values from 0 to 1
- panels: bfloat16 [16, 2, 1024, 1024], P(('cfg', 'tm'), None, 'space'), parts along dimension 0, may hold values from -6 to 6
Outputs:
- dressed: bfloat16 [16, 3, 2, 1024, 1024], P(('cfg', 'tm'), None, None, 'space'), parts along dimension 0
There are 2 independent parts, one for each index of `cfg`. A program takes and returns all parts, laid end to end along the dimension named above; an argument that names none is the same for every part. Nothing has to cross between parts.
Inputs may be any that keep to these rules, and one draw needn't show every extreme that they name: `momenta`: the first component of every momentum is nonzero.
All inputs are finite; a program needn't handle non-finite values.
Results may differ from a plain program's by a relative error of at most 0.0075.
Values may be sent and summed in bfloat16 or wider, within the bound.
A program may use at most 64 MiB of HBM per device.

v0:
```python
import math
import jax
import jax.numpy as jnp
from jax import lax
from jax.sharding import PartitionSpec as P

LX = 64


def phased_block(cosine, sine_part, real_part, imag_part):
    cos_col = cosine[:, None]
    sin_col = sine_part[:, None]
    wave_re = cos_col * real_part + sin_col * imag_part
    wave_im = cos_col * imag_part - sin_col * real_part
    upper = jnp.concatenate([wave_re, wave_im], -1)
    lower = jnp.concatenate([wave_im, -wave_re], -1)
    return jnp.stack([upper, lower], -4).astype(jnp.bfloat16)


def local(eigvecs, momenta, pair_list, panels):
    slice_count, _, colors, slab_sites, vectors = eigvecs.shape
    mom_count = momenta.shape[0]
    space_count = lax.axis_size("space")
    first_site = lax.axis_index("space") * slab_sites
    site_index = first_site + jnp.arange(slab_sites, dtype=jnp.int32)
    xpos = site_index % LX
    ypos = site_index // LX % LX
    zpos = site_index // (LX * LX)
    wave = (
        momenta[:, 0:1] * xpos[None, :]
        + momenta[:, 1:2] * ypos[None, :]
        + momenta[:, 2:3] * zpos[None, :]
    )
    wave = jnp.mod(wave, LX)
    angle = wave.astype(jnp.float32) * jnp.float32(2.0 * math.pi / LX)
    cosine = jnp.cos(angle)
    sine_part = jnp.sin(angle)
    factor = 1.0 / math.sqrt(6.0 * slab_sites * space_count * vectors)
    real_part = eigvecs[:, 0].astype(jnp.float32)
    imag_part = eigvecs[:, 1].astype(jnp.float32)
    phased_all = jnp.concatenate(
        [
            phased_block(cosine[moment], sine_part[moment], real_part, imag_part)
            for moment in range(mom_count)
        ],
        -1,
    )
    phased_all = phased_all.reshape(slice_count, 2, colors, slab_sites, mom_count, 2 * vectors)
    gram_local = jnp.einsum(
        "trcsk,trcsml->tmkl", eigvecs, phased_all, preferred_element_type=jnp.float32
    )
    gram_local = factor * gram_local
    summed = lax.psum(gram_local, "space")
    own_fields = summed.astype(jnp.bfloat16)
    meson_fields = lax.all_gather(own_fields, "tm", axis=0, tiled=True)
    pair_count = pair_list.shape[0]
    panel_rows = panels.shape[2]
    panel_width = panels.shape[3]
    spins = panel_width // vectors
    source_fields = jnp.take(meson_fields, pair_list[:, 0], axis=0).reshape(
        pair_count, mom_count, vectors, 2, vectors
    )
    sink_fields = jnp.take(meson_fields, pair_list[:, 1], axis=0).reshape(
        pair_count, mom_count, vectors, 2, vectors
    )
    panel_parts = panels.reshape(pair_count, 2, panel_rows, spins, vectors)
    panel_re = panel_parts[:, 0]
    panel_im = panel_parts[:, 1]
    panel_mix = jnp.stack(
        [jnp.stack([panel_re, panel_im], 1), jnp.stack([panel_im, -panel_re], 1)], 1
    )
    right_dressed = jnp.einsum(
        "porxbk,pmlrk->pmoxbl", panel_mix, source_fields, preferred_element_type=jnp.float32
    )
    right_dressed = right_dressed.astype(jnp.bfloat16).reshape(
        pair_count * mom_count, 2, panel_rows, panel_width
    )
    turned = lax.all_to_all(right_dressed, "space", split_axis=3, concat_axis=2, tiled=True)
    column_count = turned.shape[3]
    turned = turned.reshape(pair_count, mom_count, 2, spins, vectors, column_count)
    turned_re = turned[:, :, 0]
    turned_im = turned[:, :, 1]
    mixed_parts = jnp.stack(
        [jnp.stack([turned_re, -turned_im], 2), jnp.stack([turned_im, turned_re], 2)], 2
    )
    dressed = jnp.einsum(
        "pmorajc,pmkrj->pmocak", mixed_parts, sink_fields, preferred_element_type=jnp.float32
    )
    return dressed.reshape(pair_count, mom_count, 2, column_count, panel_width).astype(jnp.bfloat16)


def solution(mesh):
    placed = (
        P(("cfg", "tm"), None, None, "space", None),
        P(),
        P("tm", None),
        P(("cfg", "tm"), None, "space", None),
    )
    return jax.shard_map(
        local,
        mesh=mesh,
        in_specs=placed,
        out_specs=P(("cfg", "tm"), None, None, "space", None),
        check_vma=False,
    )
```

profile of v0, /device:TPU:0, one launch (start us, length us, event | category | flops | bytes accessed | tf_op | source)
XLA Modules:
  0.0 343.8 jit_solution(5193341892418195743)
XLA Ops:
  6.5 0.0 all-gather.2.cloned.1.call-start
  6.6 1.0 slice_reduce_fusion.2
  7.6 0.1 fusion.37
  7.7 0.0 copy-start.3
  7.8 1.6 fusion.30
  9.3 0.1 maximum_bitcast_fusion.9
  9.4 0.1 pad_maximum_fusion
  9.5 0.0 copy-done.3
  9.6 0.3 fusion.28
  9.8 0.1 maximum_bitcast_fusion.11
  10.0 0.1 maximum_bitcast_fusion.13
  10.1 1.2 fusion.17
  11.3 83.3 %all-reduce.1 = bf16[1,3,256,512]{2,3,1,0:T(8,128)(2,1)S(1)} all-reduce(f32[1,3,256,512]{2,3,1,0:T(8,128)S(1)} %fusion.17), channel_id=1, replica_groups=mesh['cfg'=2,'space'=8,'tm'=2] {'space'}, use_global_device_ids=true, to_apply=%region_0.1 | all-reduce | flops 393216 | bytes 2359296 | tf_op jit(solution)/shard_map/psum | solution.py:53
  94.7 1.3 copy.48
  95.9 0.0 all-gather.2.cloned.1.call-update
  95.9 3.0 copy.49
  99.0 1.5 fusion.42
  100.4 1.5 copy.77
  102.0 1.2 neg.44
  103.2 0.0 copy-start.4
  103.2 0.0 copy-start.2
  103.2 2.4 copy.76
  105.6 2.3 copy.53
  107.9 0.0 copy-done.4
  107.9 0.0 copy-done.2
  107.9 2.7 maximum_bitcast_fusion.6
  110.7 0.0 all-gather.2.cloned.1.call-done
  110.7 2.2 gather_fusion.1
  112.8 2.0 broadcast_select_fusion
  114.9 3.8 %reshape.415 = bf16[4,3,256,2,256]{4,3,2,1,0:T(2,128)(2,1)S(1)} reshape(bf16[4,3,256,512]{3,2,1,0:T(8,128)(2,1)} %broadcast_select_fusion) | data formatting | bytes 6291456 | tf_op jit(solution)/shard_map/reshape | solution.py:60
  118.6 6.2 %bitcast_convert_fusion.1 = bf16[4,3,256,2,128,4]{4,2,5,3,1,0:T(8,128)(2,1)S(1)} fusion(bf16[4,1,2,128,4,256]{5,3,2,4,1,0:T(8,128)(2,1)} %maximum_bitcast_fusion.6, bf16[4,1,2,128,4,256]{5,3,2,4,1,0:T(8,128)(2,1)} %copy.53, bf16[4,3,256,2,256,1,1]{4,3,2,1,0,6,5:T(2,128)(2,1)S(1)} %bitcast.120), kind=kOutput, calls=%fused_computation.7 | convolution fusion | flops 3232759808 | bytes 13631488 | tf_op jit(solution)/shard_map/porxbk,pmlrk->pmoxbl/dot_general | solution.py:72
  124.8 36.6 %copy.55 = bf16[12,2,128,1024]{2,1,0,3:T(2,128)(2,1)} copy(bf16[12,2,128,1024]{2,3,1,0:T(8,128)(2,1)S(1)} %bitcast.117) | data formatting | bytes 12582912 | tf_op jit(solution)/shard_map/reshape | solution.py:75
  161.5 0.0 copy-start.1
  161.5 5.1 %all-to-all-start = ((bf16[12,2,128,1024]{2,1,0,3:T(2,128)(2,1)}), bf16[12,2,128,1024]{2,1,0,3:T(2,128)(2,1)}, u32[]{:S(2)}, u32[]{:S(2)}) async-start(bf16[12,2,128,1024]{2,1,0,3:T(2,128)(2,1)} %copy.55), calls=%async_computation | async-start | bytes 12582912 | tf_op jit(solution)/shard_map/all_to_all | solution.py:78
  166.5 0.0 copy-done.1
  166.6 2.5 gather_fusion
  169.0 2.3 broadcast_select_fusion.1
  171.3 3.1 reshape.414
  174.3 125.2 %all-to-all-done = bf16[12,2,128,1024]{2,1,0,3:T(2,128)(2,1)} async-done(((bf16[12,2,128,1024]{2,1,0,3:T(2,128)(2,1)}), bf16[12,2,128,1024]{2,1,0,3:T(2,128)(2,1)}, u32[]{:S(2)}, u32[]{:S(2)}) %all-to-all-start) | async-done | bytes 6291488 | tf_op jit(solution)/shard_map/all_to_all | solution.py:78
  299.6 6.9 %copy.56 = bf16[12,2,128,1024]{2,3,1,0:T(8,128)(2,1)} copy(bf16[12,2,128,1024]{2,1,0,3:T(2,128)(2,1)} %all-to-all-done) | data formatting | bytes 12582912 | tf_op jit(solution)/shard_map/all_to_all | solution.py:78
  306.4 8.6 %copy.57 = bf16[12,2,8,128,128]{4,3,2,1,0:T(8,128)(2,1)} copy(bf16[12,2,8,128,128]{3,4,2,1,0:T(8,128)(2,1)} %bitcast.114) | data formatting | bytes 12582912 | tf_op jit(solution)/shard_map/all_to_all | solution.py:78
  315.1 0.0 copy-start
  315.1 3.4 slice_bitcast_fusion
  318.5 1.2 copy-done
  319.7 0.4 fusion.41
  320.1 1.0 maximum_bitcast_fusion
  321.1 7.2 %bitcast_convert_fusion = bf16[4,3,256,2,4,128]{5,2,4,3,1,0:T(8,128)(2,1)} fusion(bf16[4,3,1,2,4,256,128]{6,5,3,4,2,1,0:T(8,128)(2,1)S(1)} %get-tuple-element.16, bf16[4,3,1,2,4,256,128]{6,5,3,4,2,1,0:T(8,128)(2,1)S(1)} %get-tuple-element.15, bf16[4,3,256,2,256,1,1]{4,3,2,1,0,6,5:T(2,128)(2,1)} %bitcast.119), kind=kOutput, calls=%fused_computation.6 | convolution fusion | flops 3249537024 | bytes 22020096 | tf_op jit(solution)/shard_map/pmorajc,pmkrj->pmocak/dot_general | solution.py:86
  328.3 8.6 %copy.62 = bf16[4,3,2,128,1024]{4,3,2,1,0:T(8,128)(2,1)} copy(bf16[4,3,2,128,1024]{3,4,2,1,0:T(8,128)(2,1)} %bitcast.118) | data formatting | bytes 12582912 | tf_op jit(solution)/shard_map/convert_element_type | solution.py:89
  (6 shorter events, 0.1 us)
Async XLA Ops:
  6.5 104.1 %all-gather.2.cloned.1.call-start = ((), (), s32[]{:S(2)}) async-start(), calls=%async_computation.1 | async-start | bytes 2359296 | tf_op jit(solution)/shard_map/all_gather | solution.py:55
  7.7 1.8 copy-start.3
  103.2 4.7 %copy-start.4 = (s32[4,2]{0,1:T(2,128)S(1)}, s32[4,2]{0,1:T(2,128)}, u32[]{:S(2)}) copy-start(s32[4,2]{0,1:T(2,128)} %param.8) | copy-start | bytes 100
  103.2 4.7 %copy-start.2 = (bf16[4,1,128,4,256]{4,2,1,3,0:T(8,128)(2,1)S(1)}, bf16[4,1,128,4,256]{4,2,1,3,0:T(8,128)(2,1)}, u32[]{:S(2)}) copy-start(bf16[4,1,128,4,256]{4,2,1,3,0:T(8,128)(2,1)} %neg.44) | copy-start | bytes 3145732
  161.5 5.1 %copy-start.1 = (bf16[2,3,256,512]{3,2,1,0:T(8,128)(2,1)S(1)}, bf16[2,3,256,512]{3,2,1,0:T(8,128)(2,1)}, u32[]{:S(2)}) copy-start(bf16[2,3,256,512]{3,2,1,0:T(8,128)(2,1)} %all-gather.2.cloned.1.call-done) | copy-start | bytes 4718596
  161.5 138.1 %all-to-all-start = ((bf16[12,2,128,1024]{2,1,0,3:T(2,128)(2,1)}), bf16[12,2,128,1024]{2,1,0,3:T(2,128)(2,1)}, u32[]{:S(2)}, u32[]{:S(2)}) async-start(bf16[12,2,128,1024]{2,1,0,3:T(2,128)(2,1)} %copy.55), calls=%async_computation | async-start | bytes 12582912 | tf_op jit(solution)/shard_map/all_to_all | solution.py:78
  315.1 4.6 %copy-start = (bf16[12,2,8,128,128]{4,3,2,1,0:T(8,128)(2,1)S(1)}, bf16[12,2,8,128,128]{4,3,2,1,0:T(8,128)(2,1)}, u32[]{:S(2)}) copy-start(bf16[12,2,8,128,128]{4,3,2,1,0:T(8,128)(2,1)} %copy.57) | copy-start | bytes 18874372
Sparse Core Ops, SparseCore 0:
  96.1 7.9 all-gather.1
where the time goes:
time: 345 us; the launch traced here: 344 us
  waiting for transfers between devices  125 us (36%)
  local copies, waits for them, and re-layouts  89.8 us (26%)
  blocking collectives  83.3 us (24%)
  matrix products  14.6 us (4%)
  between operations  13.6 us (4%)
  other arithmetic  12 us (3%)
  starting transfers between devices  5.08 us (1%)
    all_to_all x1, waiting for transfers between devices, local(): lax.all_to_all(right_dressed, 'space', split_axis=3, concat_axis=2, tiled...  125 us
    psum x1, blocking collectives, local(): summed = lax.psum(gram_local, 'space')  83.3 us
    reshape x1, local copies, waits for them, and re-layouts, local(): right_dressed.astype(jnp.bfloat16)  36.6 us
    all_to_all x2, local copies, waits for them, and re-layouts, local(): lax.all_to_all(right_dressed, 'space', split_axis=3, concat_axis=2, tiled...  15.5 us
    unnamed x14, local copies, waits for them, and re-layouts  11.6 us
    convert_element_type x1, local copies, waits for them, and re-layouts, local(): dressed.reshape(pair_count, mom_count, 2, column_count, panel_width)  8.62 us
    dot_general x1, matrix products, local(): jnp.einsum('pmorajc,pmkrj->pmocak', mixed_parts, sink_fields, preferred_e...  7.2 us
  transfers between devices with their start and end apart: 2, of which 1 were waited for; matrix products, arithmetic and copies ran while one was open for 7% of the time, Pallas kernels for 0%

commit v1 on v0

--- a/solution.py
+++ b/solution.py
@@ -50,7 +50,8 @@
         "trcsk,trcsml->tmkl", eigvecs, phased_all, preferred_element_type=jnp.float32
     )
     gram_local = factor * gram_local
-    summed = lax.psum(gram_local, "space")
+    shards = lax.all_gather(gram_local, "space", axis=0, tiled=False)
+    summed = shards.sum(axis=0)
     own_fields = summed.astype(jnp.bfloat16)
     meson_fields = lax.all_gather(own_fields, "tm", axis=0, tiled=True)
     pair_count = pair_list.shape[0]

time: 345 us -> 453 us (1.31)
  waiting for transfers between devices: 125 us -> 309 us
  blocking collectives: 83.3 us -> 0 us
  other arithmetic: 12 us -> 18.4 us
    all_gather x0 -> x1, waiting for transfers between devices: none -> 179 us  [local(): shards = lax.all_gather(gram_local, 'space', axis=0, tiled=False)]
    psum x1 -> x0, blocking collectives: 83.3 us -> none  [local(): summed = lax.psum(gram_local, 'space')]
    reshape x2 -> x0, local copies, waits for them, and re-layouts: 6.8 us -> none  [the longest x1 3.75 us: local(): jnp.take(meson_fields, pair_list[:, 0], axis=0)]
    reduce_sum x0 -> x1, other arithmetic: none -> 6.3 us  [local(): summed = shards.sum(axis=0)]
    select_n x0 -> x2, local copies, waits for them, and re-layouts: none -> 6.04 us  [the longest x1 3.17 us: local(): jnp.take(meson_fields, pair_list[:, 0], axis=0)]
    all_to_all x1, waiting for transfers between devices: 125 us -> 130 us  [local(): lax.all_to_all(right_dressed, 'space', split_axis=3, concat_axis=2, tiled...]
    unnamed x14 -> x15, local copies, waits for them, and re-layouts: 11.6 us -> 11.8 us
  transfers between devices with their start and end apart: 2 -> 3, of which waited for: 1 -> 2; matrix products, arithmetic and copies ran while one was open for 7% -> 5% of each run, Pallas kernels for 0% -> 0%
where the time goes in v1:
time: 453 us; the launch traced here: 452 us
  waiting for transfers between devices  309 us (68%)
  local copies, waits for them, and re-layouts  91 us (20%)
  other arithmetic  18.4 us (4%)
  matrix products  14.9 us (3%)
  between operations  13.6 us (3%)
  starting transfers between devices  5.34 us (1%)
    all_gather x1, waiting for transfers between devices, local(): shards = lax.all_gather(gram_local, 'space', axis=0, tiled=False)  179 us
    all_to_all x1, waiting for transfers between devices, local(): lax.all_to_all(right_dressed, 'space', split_axis=3, concat_axis=2, tiled...  130 us
    reshape x1, local copies, waits for them, and re-layouts, local(): right_dressed.astype(jnp.bfloat16)  36.6 us
    all_to_all x2, local copies, waits for them, and re-layouts, local(): lax.all_to_all(right_dressed, 'space', split_axis=3, concat_axis=2, tiled...  15.5 us
    unnamed x15, local copies, waits for them, and re-layouts  11.8 us
  transfers between devices with their start and end apart: 3, of which 2 were waited for; matrix products, arithmetic and copies ran while one was open for 5% of the time, Pallas kernels for 0%

profile of v1, /device:TPU:0, one launch (start us, length us, event | category | flops | bytes accessed | tf_op | source)
XLA Modules:
  0.0 452.0 jit_solution(7735838509833685711)
XLA Ops:
  6.5 0.0 all-gather.5.cloned.1.call-start
  6.6 1.0 slice_reduce_fusion.2
  7.6 0.1 fusion.35
  7.7 0.0 copy-start.3
  7.8 1.6 fusion.28
  9.3 0.1 maximum_bitcast_fusion.9
  9.4 0.1 pad_maximum_fusion
  9.5 0.0 copy-done.3
  9.6 0.3 fusion.26
  9.8 0.1 maximum_bitcast_fusion.11
  10.0 0.1 maximum_bitcast_fusion.13
  10.1 1.2 fusion.15
  11.3 1.6 copy.48
  12.9 0.0 all-gather.5.cloned.1.call-update
  12.9 0.2 all-gather.7.cloned.1.call-start
  13.2 178.7 %all-gather.5.cloned.1.call-done = f32[8,3,256,512]{3,2,1,0:T(8,128)} async-done(((f32[1,3,256,512]{3,2,1,0:T(8,128)}), f32[8,3,256,512]{3,2,1,0:T(8,128)}) %all-gather.5.cloned.1.call-update) | async-done | bytes 12582928 | tf_op jit(solution)/shard_map/all_gather | solution.py:53
  191.9 6.3 %reduce.1 = bf16[3,256,512]{2,1,0:T(8,128)(2,1)S(1)} reduce(f32[8,3,256,512]{3,2,1,0:T(8,128)} %all-gather.5.cloned.1.call-done, f32[]{:T(128)} %constant.75.clone.1), dimensions={0}, to_apply=%region_0.1 | reduce | flops 2752512 | bytes 13369348 | tf_op jit(solution)/shard_map/reduce_sum | solution.py:54
  198.2 0.3 copy.80
  198.5 1.2 copy.50
  199.7 0.0 all-gather.7.cloned.1.call-update
  199.8 3.0 copy.53
  202.8 1.5 fusion.40
  204.3 1.5 copy.82
  205.8 1.2 neg.44
  207.0 2.4 copy.81
  209.4 2.4 copy.57
  211.8 0.0 copy-done.4
  211.8 0.0 copy-done.2
  211.8 2.8 maximum_bitcast_fusion.6
  214.6 2.2 gather_fusion.1
  216.7 2.0 broadcast_select_fusion
  218.7 3.2 copy.52
  221.9 6.4 %bitcast_convert_fusion.1 = bf16[4,3,256,2,128,4]{4,2,5,3,1,0:T(8,128)(2,1)S(1)} fusion(bf16[4,3,256,2,256,1,1]{2,4,3,6,5,1,0:T(8,128)(2,1)S(1)} %bitcast.129, bf16[4,1,2,128,4,256]{5,3,2,4,1,0:T(8,128)(2,1)} %maximum_bitcast_fusion.6, bf16[4,1,2,128,4,256]{5,3,2,4,1,0:T(8,128)(2,1)} %copy.57), kind=kOutput, calls=%fused_computation.7 | convolution fusion | flops 3232759808 | bytes 13631488 | tf_op jit(solution)/shard_map/porxbk,pmlrk->pmoxbl/dot_general | solution.py:73
  228.3 36.6 %copy.59 = bf16[12,2,128,1024]{2,1,0,3:T(2,128)(2,1)} copy(bf16[12,2,128,1024]{2,3,1,0:T(8,128)(2,1)S(1)} %bitcast.126) | data formatting | bytes 12582912 | tf_op jit(solution)/shard_map/reshape | solution.py:76
  264.9 5.1 %all-to-all-start = ((bf16[12,2,128,1024]{2,1,0,3:T(2,128)(2,1)}), bf16[12,2,128,1024]{2,1,0,3:T(2,128)(2,1)}, u32[]{:S(2)}, u32[]{:S(2)}) async-start(bf16[12,2,128,1024]{2,1,0,3:T(2,128)(2,1)} %copy.59), calls=%async_computation | async-start | bytes 12582912 | tf_op jit(solution)/shard_map/all_to_all | solution.py:79
  270.0 0.0 copy-done.1
  270.0 2.5 gather_fusion
  272.5 2.3 broadcast_select_fusion.1
  274.8 2.9 copy.51
  277.6 130.0 %all-to-all-done = bf16[12,2,128,1024]{2,1,0,3:T(2,128)(2,1)} async-done(((bf16[12,2,128,1024]{2,1,0,3:T(2,128)(2,1)}), bf16[12,2,128,1024]{2,1,0,3:T(2,128)(2,1)}, u32[]{:S(2)}, u32[]{:S(2)}) %all-to-all-start) | async-done | bytes 6291488 | tf_op jit(solution)/shard_map/all_to_all | solution.py:79
  407.7 6.9 %copy.60 = bf16[12,2,128,1024]{2,3,1,0:T(8,128)(2,1)} copy(bf16[12,2,128,1024]{2,1,0,3:T(2,128)(2,1)} %all-to-all-done) | data formatting | bytes 12582912 | tf_op jit(solution)/shard_map/all_to_all | solution.py:79
  414.5 8.7 %copy.61 = bf16[12,2,8,128,128]{4,3,2,1,0:T(8,128)(2,1)} copy(bf16[12,2,8,128,128]{3,4,2,1,0:T(8,128)(2,1)} %bitcast.121) | data formatting | bytes 12582912 | tf_op jit(solution)/shard_map/all_to_all | solution.py:79
  423.2 3.4 slice_bitcast_fusion
  426.6 1.2 copy-done
  427.8 0.4 fusion.39
  428.2 1.0 maximum_bitcast_fusion
  429.2 7.3 %bitcast_convert_fusion = bf16[4,3,256,2,4,128]{5,2,4,3,1,0:T(8,128)(2,1)} fusion(bf16[4,3,256,2,256,1,1]{2,4,3,6,5,1,0:T(8,128)(2,1)} %bitcast.128, bf16[4,3,1,2,4,256,128]{6,5,3,4,2,1,0:T(8,128)(2,1)S(1)} %get-tuple-element.16, bf16[4,3,1,2,4,256,128]{6,5,3,4,2,1,0:T(8,128)(2,1)S(1)} %get-tuple-element.15), kind=kOutput, calls=%fused_computation.6 | convolution fusion | flops 3249537024 | bytes 22020096 | tf_op jit(solution)/shard_map/pmorajc,pmkrj->pmocak/dot_general | solution.py:87
  436.6 8.6 %copy.66 = bf16[4,3,2,128,1024]{4,3,2,1,0:T(8,128)(2,1)} copy(bf16[4,3,2,128,1024]{3,4,2,1,0:T(8,128)(2,1)} %bitcast.127) | data formatting | bytes 12582912 | tf_op jit(solution)/shard_map/convert_element_type | solution.py:90
  (11 shorter events, 0.1 us)
Async XLA Ops:
  6.5 185.4 %all-gather.5.cloned.1.call-start = ((), (), s32[]{:S(2)}) async-start(), calls=%async_computation.1 | async-start | bytes 14155776 | tf_op jit(solution)/shard_map/all_gather | solution.py:53
  7.7 1.8 copy-start.3
  12.9 201.6 %all-gather.7.cloned.1.call-start = ((), (), s32[]{:S(2)}) async-start(), calls=%async_computation.2 | async-start | bytes 2359296 | tf_op jit(solution)/shard_map/all_gather | solution.py:56
  207.0 4.7 %copy-start.4 = (s32[4,2]{0,1:T(2,128)S(1)}, s32[4,2]{0,1:T(2,128)}, u32[]{:S(2)}) copy-start(s32[4,2]{0,1:T(2,128)} %param.8) | copy-start | bytes 100
  207.0 4.8 %copy-start.2 = (bf16[4,1,128,4,256]{4,2,1,3,0:T(8,128)(2,1)S(1)}, bf16[4,1,128,4,256]{4,2,1,3,0:T(8,128)(2,1)}, u32[]{:S(2)}) copy-start(bf16[4,1,128,4,256]{4,2,1,3,0:T(8,128)(2,1)} %neg.44) | copy-start | bytes 3145732
  264.9 5.1 %copy-start.1 = (bf16[6,256,512]{2,1,0:T(8,128)(2,1)S(1)}, bf16[6,256,512]{2,1,0:T(8,128)(2,1)}, u32[]{:S(2)}) copy-start(bf16[6,256,512]{2,1,0:T(8,128)(2,1)} %all-gather.7.cloned.1.call-done) | copy-start | bytes 4718596
  264.9 142.7 %all-to-all-start = ((bf16[12,2,128,1024]{2,1,0,3:T(2,128)(2,1)}), bf16[12,2,128,1024]{2,1,0,3:T(2,128)(2,1)}, u32[]{:S(2)}, u32[]{:S(2)}) async-start(bf16[12,2,128,1024]{2,1,0,3:T(2,128)(2,1)} %copy.59), calls=%async_computation | async-start | bytes 12582912 | tf_op jit(solution)/shard_map/all_to_all | solution.py:79
  423.2 4.6 %copy-start = (bf16[12,2,8,128,128]{4,3,2,1,0:T(8,128)(2,1)S(1)}, bf16[12,2,8,128,128]{4,3,2,1,0:T(8,128)(2,1)}, u32[]{:S(2)}) copy-start(bf16[12,2,8,128,128]{4,3,2,1,0:T(8,128)(2,1)} %copy.61) | copy-start | bytes 18874372
Sparse Core Ops, SparseCore 0:
  13.1 178.8 all-gather.4
  199.9 7.9 all-gather.6
